TPU v7x, 128 devices: a whole 4x4x4 slice. The times are simulated.
128 devices in a mesh: band: 4 (over x_hi, core), feed: 32 (over y, z, x_lo).
Axes of the slice: x: 4 (x_hi: 2, x_lo: 2; x = x_hi * 2 + x_lo), y: 4, z: 4, core: 2. Of those that a mesh axis runs over, the one named last changes fastest.
Arguments:
- voltages: float32 [768, 2048, 128], P('band', 'feed'), may hold values from -6 to 6
- feed_cells: int32 [4096], replicated, may hold values from 0 to 4095, each once
- delays: int32 [768, 256], P('band'), may hold values from 0 to 63
Outputs:
- dedispersed: float32 [256, 1024, 64], P('band', 'feed')
Inputs may be any that keep to these rules, and one draw needn't show every extreme that they name: `feed_cells`: a permutation of the cells of the 64 x 64 feed grid, so no two feeds share a cell.
All inputs are finite; a program needn't handle non-finite values.
Results may differ from a plain program's by a relative error of at most 0.0003.
Values sent between devices are 32-bit elements; how exact they have to be, the bound alone decides.
A program may use at most 128 MiB of HBM per device.

v0:
```python
import math

import jax
import jax.numpy as jnp
from jax import lax
from jax.sharding import PartitionSpec as P

FEEDS = 2048
CHANNELS = 768
FRAMES = 64
SIDE = 32
BEAMS = 1024
GRID = 64


def cut_along(x, dim, peers):
    dims = x.shape
    pieces = x.reshape(*dims[:dim], peers, dims[dim] // peers, *dims[dim + 1 :])
    return jnp.moveaxis(pieces, dim, 0)


def piece_ends(length, count):
    unit = 8 if length >= 8 * count else 1
    return [length // unit * k // count * unit for k in range(1, count)]


def laid_out(pieces, dim):
    pieces = jnp.moveaxis(pieces, 0, dim)
    dims = pieces.shape
    return pieces.reshape(*dims[:dim], dims[dim] * dims[dim + 1], *dims[dim + 2 :])


def exchange_in_pieces(x, axis, pieces, split_dim, concat_dim):
    blocks = cut_along(x, split_dim, lax.axis_size(axis))
    widest = max(range(1, max(2, blocks.ndim - 1)), key=lambda d: blocks.shape[d])
    outs = []
    for slab in jnp.split(blocks, piece_ends(blocks.shape[widest], pieces), axis=widest):
        if slab.size:
            outs.append(lax.all_to_all(slab, axis, split_axis=0, concat_axis=0, tiled=True))
    return laid_out(jnp.concatenate(outs, axis=widest), concat_dim)


def sum_at_owner(x, axis, dim):
    peers = lax.axis_size(axis)
    pieces = lax.all_to_all(cut_along(x, dim, peers), axis, 0, 0, tiled=True)
    return jnp.sum(pieces, axis=0)


def feed_offsets(feed_cells):
    cell_index = feed_cells[:FEEDS]
    cell_row = cell_index // GRID
    cell_col = cell_index % GRID
    beam_ids = jnp.arange(BEAMS, dtype=jnp.int32)
    beam_row = beam_ids // SIDE - SIDE // 2
    beam_col = beam_ids % SIDE - SIDE // 2
    return beam_row[:, None] * cell_row[None, :] + beam_col[:, None] * cell_col[None, :]


def steering(offsets, channel):
    residue = jnp.mod(offsets * (CHANNELS + channel), GRID * CHANNELS)
    phases = residue.astype(jnp.float32) * (2.0 * math.pi / (GRID * CHANNELS))
    factor = 1.0 / math.sqrt(FEEDS)
    return (jnp.cos(phases) * factor, jnp.sin(phases) * factor)


def frame_tables():
    frame_ids = jnp.arange(FRAMES, dtype=jnp.int32)
    wave = jnp.mod(frame_ids[:, None] * frame_ids[None, :], FRAMES).astype(jnp.float32) * (
        2.0 * math.pi / FRAMES
    )
    nonzero = (frame_ids > 0).astype(jnp.float32)[None, :]
    forward = jnp.concatenate([jnp.cos(wave) * nonzero, -jnp.sin(wave) * nonzero], axis=1)
    inverse = jnp.concatenate([jnp.cos(wave), -jnp.sin(wave)], axis=0) * (
        0.5 / (FRAMES * math.sqrt(CHANNELS))
    )
    return (frame_ids, forward, inverse)


def to_spectra(by_beam, chan_count, forward):
    beams_here = by_beam.shape[1] // FRAMES
    spectra = jnp.dot(
        by_beam.reshape(chan_count * beams_here, FRAMES), forward, precision=lax.Precision.HIGHEST
    )
    spectra = spectra.reshape(chan_count, beams_here, 2 * FRAMES)
    return (spectra[:, :, :FRAMES], spectra[:, :, FRAMES:])


def shifted_rows(spec_real, spec_imag, table, frame_ids):
    highest = lax.Precision.HIGHEST
    residue = jnp.mod(frame_ids[:, None, None] * table[None, :, :], FRAMES)
    phases = residue.astype(jnp.float32) * (2.0 * math.pi / FRAMES)
    shift_cos = jnp.cos(phases)
    shift_sin = jnp.sin(phases)
    out_real = jnp.einsum("kcd,cbk->dbk", shift_cos, spec_real, precision=highest)
    out_real = out_real - jnp.einsum("kcd,cbk->dbk", shift_sin, spec_imag, precision=highest)
    out_imag = jnp.einsum("kcd,cbk->dbk", shift_cos, spec_imag, precision=highest)
    out_imag = out_imag + jnp.einsum("kcd,cbk->dbk", shift_sin, spec_real, precision=highest)
    return jnp.concatenate([out_real, out_imag], axis=2)


def to_series(folded, inverse):
    row_count, beams_here = (folded.shape[0], folded.shape[1])
    series = jnp.dot(
        folded.reshape(row_count * beams_here, 2 * FRAMES), inverse, precision=lax.Precision.HIGHEST
    )
    return series.reshape(row_count, beams_here, FRAMES)


def body(voltages, feed_cells, delays):
    highest = lax.Precision.HIGHEST
    band_chans = voltages.shape[0]
    by_channel = exchange_in_pieces(voltages, "feed", 2, 0, 1)
    local_chans = by_channel.shape[0]
    first_chan = lax.axis_index("band") * band_chans + lax.axis_index("feed") * local_chans
    offsets = feed_offsets(feed_cells)

    def beam_power(item):
        channel, voltage = item
        cosine, sine_part = steering(offsets, channel)
        weights = jnp.concatenate([cosine, sine_part], axis=0)
        products = jnp.dot(weights, voltage, precision=highest)
        with_cos = products[:BEAMS]
        with_sin = products[BEAMS:]
        real_part = with_cos[:, :FRAMES] + with_sin[:, FRAMES:]
        imag_part = with_cos[:, FRAMES:] - with_sin[:, :FRAMES]
        return (real_part * real_part + imag_part * imag_part).reshape(BEAMS * FRAMES)

    channels = first_chan + jnp.arange(local_chans, dtype=jnp.int32)
    powers = lax.map(beam_power, (channels, by_channel))
    frame_ids, forward, inverse = frame_tables()
    by_beam = lax.all_to_all(powers, "feed", split_axis=1, concat_axis=0, tiled=True)
    spec_real, spec_imag = to_spectra(by_beam, band_chans, forward)
    return sum_at_owner(
        to_series(shifted_rows(spec_real, spec_imag, delays, frame_ids), inverse), "band", 0
    )


def solution(mesh):
    placed = (P("band", "feed", None), P(), P("band", None))
    return jax.shard_map(
        body, mesh=mesh, in_specs=placed, out_specs=P("band", "feed", None), check_vma=False
    )
```

profile of v0, /device:TPU:1, one launch (start us, length us, event | category | flops | bytes accessed | tf_op | source)
XLA Modules:
  0.0 857.4 jit_solution(10615475838807271146)
XLA Ops:
  0.0 5.5 fusion.85
  5.5 49.1 %all_to_all.31 = f32[32,6,32,128]{3,2,1,0:T(8,128)S(1)} all-to-all(f32[32,6,32,128]{3,2,1,0:T(8,128)S(1)} %get-tuple-element.114), channel_id=1, replica_groups=mesh['band'=4,'feed'=32] {'feed'}, dimensions={0} | all-to-all | bytes 6291456 | tf_op jit(solution)/shard_map/all_to_all | solution.py:39
  54.6 4.8 all-to-all-start.1
  59.5 44.6 %all-to-all-done.1 = f32[32,6,32,128]{3,2,1,0:T(8,128)} async-done(((f32[32,6,32,128]{3,2,1,0:T(8,128)}), f32[32,6,32,128]{3,2,1,0:T(8,128)}, u32[]{:S(2)}, u32[]{:S(2)}) %all-to-all-start.1) | async-done | bytes 3145760 | tf_op jit(solution)/shard_map/all_to_all | solution.py:39
  104.1 2.6 pad_maximum_fusion
  106.7 3.3 copy.53
  110.0 409.4 %while.13 = (s32[]{:T(128)}, f32[6,65536]{1,0:T(8,128)}, s32[6]{0:T(128)S(1)}, f32[6,2048,128]{2,1,0:T(8,128)}, s32[2048]{0:T(1024)S(1)}, /*index=5*/s32[1024]{0...) while((s32[]{:T(128)}, f32[6,65536]{1,0:T(8,128)}, ...), condition=%wide.region_1.2_spmd.clone, body=%wide.region_0.1_spmd.clone.sunk | while | flops 6476333056 | bytes 38560396 | solution.py:129
  110.4 0.6 dynamic_slice.23
  111.6 36.8 %cosine_multiply_fusion.2 = (f32[1024,2048]{1,0:T(8,128)S(1)}, f32[1024,2048]{1,0:T(8,128)}) fusion(s32[]{:T(128)} %bitcast.37, s32[2048]{0:T(1024)S(1)} %get-tuple-element.205, s32[1024]{0:T(1024)S(1)} %get-tuple-element.206, s32[2048]{0:T(1024)S(1)} %get-tuple-element.203, s32[1024]{0:T(1024)S(1)} %get-tuple-element.204), kind=kLoop, calls=%fused_computation.13.clone.1 | loop fusion | flops 29360128 | bytes 16801796 | tf_op jit(solution)/shard_map/while/body/eval_jaxpr/mul | solution.py:63
  148.4 21.1 %fusion.108 = f32[2048,128]{0,1:T(8,128)S(1)} fusion(f32[1024,2048]{1,0:T(8,128)} %get-tuple-element.175, f32[1024,2048]{1,0:T(8,128)S(1)} %get-tuple-element.176, f32[6,2048,128]{2,1,0:T(8,128)} %get-tuple-element.202, s32[]{:T(128)} %get-tuple-element.188), kind=kOutput, calls=%fused_computation.1.clone.1 | convolution fusion | flops 6446645248 | bytes 18874880 | tf_op jit(solution)/shard_map/while/body/eval_jaxpr/dot_general | solution.py:121
  170.1 6.0 dynamic_update_slice.9
  176.2 0.6 dynamic_slice.23
  177.4 36.8 %cosine_multiply_fusion.2 = (f32[1024,2048]{1,0:T(8,128)S(1)}, f32[1024,2048]{1,0:T(8,128)}) fusion(s32[]{:T(128)} %bitcast.37, s32[2048]{0:T(1024)S(1)} %get-tuple-element.205, s32[1024]{0:T(1024)S(1)} %get-tuple-element.206, s32[2048]{0:T(1024)S(1)} %get-tuple-element.203, s32[1024]{0:T(1024)S(1)} %get-tuple-element.204), kind=kLoop, calls=%fused_computation.13.clone.1 | loop fusion | flops 29360128 | bytes 16801796 | tf_op jit(solution)/shard_map/while/body/eval_jaxpr/mul | solution.py:63
  214.2 21.1 %fusion.108 = f32[2048,128]{0,1:T(8,128)S(1)} fusion(f32[1024,2048]{1,0:T(8,128)} %get-tuple-element.175, f32[1024,2048]{1,0:T(8,128)S(1)} %get-tuple-element.176, f32[6,2048,128]{2,1,0:T(8,128)} %get-tuple-element.202, s32[]{:T(128)} %get-tuple-element.188), kind=kOutput, calls=%fused_computation.1.clone.1 | convolution fusion | flops 6446645248 | bytes 18874880 | tf_op jit(solution)/shard_map/while/body/eval_jaxpr/dot_general | solution.py:121
  235.9 6.0 dynamic_update_slice.9
  241.9 0.6 dynamic_slice.23
  243.2 36.8 %cosine_multiply_fusion.2 = (f32[1024,2048]{1,0:T(8,128)S(1)}, f32[1024,2048]{1,0:T(8,128)}) fusion(s32[]{:T(128)} %bitcast.37, s32[2048]{0:T(1024)S(1)} %get-tuple-element.205, s32[1024]{0:T(1024)S(1)} %get-tuple-element.206, s32[2048]{0:T(1024)S(1)} %get-tuple-element.203, s32[1024]{0:T(1024)S(1)} %get-tuple-element.204), kind=kLoop, calls=%fused_computation.13.clone.1 | loop fusion | flops 29360128 | bytes 16801796 | tf_op jit(solution)/shard_map/while/body/eval_jaxpr/mul | solution.py:63
  280.0 21.1 %fusion.108 = f32[2048,128]{0,1:T(8,128)S(1)} fusion(f32[1024,2048]{1,0:T(8,128)} %get-tuple-element.175, f32[1024,2048]{1,0:T(8,128)S(1)} %get-tuple-element.176, f32[6,2048,128]{2,1,0:T(8,128)} %get-tuple-element.202, s32[]{:T(128)} %get-tuple-element.188), kind=kOutput, calls=%fused_computation.1.clone.1 | convolution fusion | flops 6446645248 | bytes 18874880 | tf_op jit(solution)/shard_map/while/body/eval_jaxpr/dot_general | solution.py:121
  301.7 6.0 dynamic_update_slice.9
  309.0 36.8 %cosine_multiply_fusion.2 = (f32[1024,2048]{1,0:T(8,128)S(1)}, f32[1024,2048]{1,0:T(8,128)}) fusion(s32[]{:T(128)} %bitcast.37, s32[2048]{0:T(1024)S(1)} %get-tuple-element.205, s32[1024]{0:T(1024)S(1)} %get-tuple-element.206, s32[2048]{0:T(1024)S(1)} %get-tuple-element.203, s32[1024]{0:T(1024)S(1)} %get-tuple-element.204), kind=kLoop, calls=%fused_computation.13.clone.1 | loop fusion | flops 29360128 | bytes 16801796 | tf_op jit(solution)/shard_map/while/body/eval_jaxpr/mul | solution.py:63
  345.8 21.1 %fusion.108 = f32[2048,128]{0,1:T(8,128)S(1)} fusion(f32[1024,2048]{1,0:T(8,128)} %get-tuple-element.175, f32[1024,2048]{1,0:T(8,128)S(1)} %get-tuple-element.176, f32[6,2048,128]{2,1,0:T(8,128)} %get-tuple-element.202, s32[]{:T(128)} %get-tuple-element.188), kind=kOutput, calls=%fused_computation.1.clone.1 | convolution fusion | flops 6446645248 | bytes 18874880 | tf_op jit(solution)/shard_map/while/body/eval_jaxpr/dot_general | solution.py:121
  367.5 6.0 dynamic_update_slice.9
  374.8 36.8 %cosine_multiply_fusion.2 = (f32[1024,2048]{1,0:T(8,128)S(1)}, f32[1024,2048]{1,0:T(8,128)}) fusion(s32[]{:T(128)} %bitcast.37, s32[2048]{0:T(1024)S(1)} %get-tuple-element.205, s32[1024]{0:T(1024)S(1)} %get-tuple-element.206, s32[2048]{0:T(1024)S(1)} %get-tuple-element.203, s32[1024]{0:T(1024)S(1)} %get-tuple-element.204), kind=kLoop, calls=%fused_computation.13.clone.1 | loop fusion | flops 29360128 | bytes 16801796 | tf_op jit(solution)/shard_map/while/body/eval_jaxpr/mul | solution.py:63
  411.6 21.1 %fusion.108 = f32[2048,128]{0,1:T(8,128)S(1)} fusion(f32[1024,2048]{1,0:T(8,128)} %get-tuple-element.175, f32[1024,2048]{1,0:T(8,128)S(1)} %get-tuple-element.176, f32[6,2048,128]{2,1,0:T(8,128)} %get-tuple-element.202, s32[]{:T(128)} %get-tuple-element.188), kind=kOutput, calls=%fused_computation.1.clone.1 | convolution fusion | flops 6446645248 | bytes 18874880 | tf_op jit(solution)/shard_map/while/body/eval_jaxpr/dot_general | solution.py:121
  433.3 6.0 dynamic_update_slice.9
  440.5 36.8 %cosine_multiply_fusion.2 = (f32[1024,2048]{1,0:T(8,128)S(1)}, f32[1024,2048]{1,0:T(8,128)}) fusion(s32[]{:T(128)} %bitcast.37, s32[2048]{0:T(1024)S(1)} %get-tuple-element.205, s32[1024]{0:T(1024)S(1)} %get-tuple-element.206, s32[2048]{0:T(1024)S(1)} %get-tuple-element.203, s32[1024]{0:T(1024)S(1)} %get-tuple-element.204), kind=kLoop, calls=%fused_computation.13.clone.1 | loop fusion | flops 29360128 | bytes 16801796 | tf_op jit(solution)/shard_map/while/body/eval_jaxpr/mul | solution.py:63
  477.4 21.1 %fusion.108 = f32[2048,128]{0,1:T(8,128)S(1)} fusion(f32[1024,2048]{1,0:T(8,128)} %get-tuple-element.175, f32[1024,2048]{1,0:T(8,128)S(1)} %get-tuple-element.176, f32[6,2048,128]{2,1,0:T(8,128)} %get-tuple-element.202, s32[]{:T(128)} %get-tuple-element.188), kind=kOutput, calls=%fused_computation.1.clone.1 | convolution fusion | flops 6446645248 | bytes 18874880 | tf_op jit(solution)/shard_map/while/body/eval_jaxpr/dot_general | solution.py:121
  499.1 6.0 dynamic_update_slice.9
  519.4 4.0 all-to-all-start.2
  523.8 28.1 %all-to-all-done.2 = f32[6,32,2048]{2,0,1:T(8,128)S(1)} async-done(((f32[6,32,2048]{2,0,1:T(8,128)}), f32[6,32,2048]{2,0,1:T(8,128)S(1)}, u32[]{:S(2)}, u32[]{:S(2)}) %all-to-all-start.2) | async-done | bytes 1572896 | tf_op jit(solution)/shard_map/all_to_all | solution.py:131
  551.9 1.3 copy-done
  553.3 2.9 dot_general.28
  556.2 2.7 fusion.39
  558.9 2.7 fusion.86
  561.6 4.6 copy.46
  566.3 3.4 copy.47
  569.6 55.1 %fusion.29 = f32[64,32,256]{2,1,0:T(8,128)S(1)} fusion(f32[192,32,64]{0,1,2:T(8,128)} %copy.46, s32[192,256]{1,0:T(8,128)S(1)} %copy-done.4), kind=kOutput, calls=%fused_computation.37 | convolution fusion | flops 1251999744 | bytes 3866624 | tf_op jit(solution)/shard_map/kcd,cbk->dbk/dot_general | solution.py:94
  624.7 54.2 %fusion.27 = f32[64,32,256]{2,1,0:T(8,128)S(1)} fusion(f32[192,32,64]{0,1,2:T(8,128)S(1)} %copy-done.2, s32[192,256]{1,0:T(8,128)S(1)} %copy-done.4), kind=kOutput, calls=%fused_computation.36 | convolution fusion | flops 1251999744 | bytes 3866624 | tf_op jit(solution)/shard_map/kcd,cbk->dbk/dot_general | solution.py:96
  678.9 54.4 %subtract_bitcast_fusion = f32[256,32,64]{0,1,2:T(8,128)S(1)} fusion(f32[64,32,256]{2,1,0:T(8,128)S(1)} %fusion.29, f32[192,32,64]{0,1,2:T(8,128)S(1)} %copy-done.2, s32[192,256]{1,0:T(8,128)S(1)} %copy-done.4), kind=kOutput, calls=%fused_computation.42 | convolution fusion | flops 1252524032 | bytes 5963776 | tf_op jit(solution)/shard_map/kcd,cbk->dbk/dot_general | solution.py:95
  733.3 54.8 %add_bitcast_fusion = f32[256,32,64]{0,1,2:T(8,128)S(1)} fusion(f32[64,32,256]{2,1,0:T(8,128)S(1)} %fusion.27, f32[192,32,64]{0,1,2:T(8,128)S(1)} %copy-done.1, s32[192,256]{1,0:T(8,128)S(1)} %copy-done.4), kind=kOutput, calls=%fused_computation.41 | convolution fusion | flops 1252524032 | bytes 5963776 | tf_op jit(solution)/shard_map/kcd,cbk->dbk/dot_general | solution.py:97
  788.0 2.3 pad_maximum_fusion.1
  790.3 5.9 copy.50
  796.2 6.8 fusion.46
  803.0 4.5 reshape.57
  807.5 33.7 %all_to_all.32 = f32[4,1,131072]{2,1,0:T(1,128)} all-to-all(f32[4,1,131072]{2,1,0:T(1,128)S(1)} %reshape.57), channel_id=1, replica_groups=mesh['band'=4,'feed'=32] {'band'}, dimensions={0} | all-to-all | bytes 4194304 | tf_op jit(solution)/shard_map/all_to_all | solution.py:45
  841.8 7.7 reduce
  849.5 3.9 reshape.58
  853.4 3.8 reduce_sum.9
  (39 shorter events, 6.2 us)
Async XLA Ops:
  5.5 54.0 %copy-start.3 = (s32[4096]{0:T(1024)S(1)}, s32[4096]{0:T(1024)}, u32[]{:S(2)}) copy-start(s32[4096]{0:T(1024)} %param.6) | copy-start | bytes 49156
  54.6 49.5 %all-to-all-start.1 = ((f32[32,6,32,128]{3,2,1,0:T(8,128)}), f32[32,6,32,128]{3,2,1,0:T(8,128)}, u32[]{:S(2)}, u32[]{:S(2)}) async-start(f32[32,6,32,128]{3,2,1,0:T(8,128)} %get-tuple-element.115), calls=%async_computation.1 | async-start | bytes 6291456 | tf_op jit(solution)/shard_map/all_to_all | solution.py:39
  519.4 32.5 %all-to-all-start.2 = ((f32[6,32,2048]{2,0,1:T(8,128)}), f32[6,32,2048]{2,0,1:T(8,128)S(1)}, u32[]{:S(2)}, u32[]{:S(2)}) async-start(f32[6,32,2048]{2,0,1:T(8,128)} %bitcast.42), calls=%async_computation.2 | async-start | bytes 4194304 | tf_op jit(solution)/shard_map/all_to_all | solution.py:131
  551.9 1.3 copy-start
  561.6 8.0 copy-start.4
  569.6 55.1 %copy-start.2 = (f32[192,32,64]{0,1,2:T(8,128)S(1)}, f32[192,32,64]{0,1,2:T(8,128)}, u32[]{:S(2)}) copy-start(f32[192,32,64]{0,1,2:T(8,128)} %copy.47) | copy-start | bytes 4718596
  678.9 54.4 %copy-start.1 = (f32[192,32,64]{0,1,2:T(8,128)S(1)}, f32[192,32,64]{0,1,2:T(8,128)}, u32[]{:S(2)}) copy-start(f32[192,32,64]{0,1,2:T(8,128)} %copy.46) | copy-start | bytes 4718596
where the time goes:
time: 862 us; the launch traced here: 857 us
  matrix products  355 us (41%)
  other arithmetic  238 us (28%)
  blocking collectives  82.8 us (10%)
  local copies, waits for them, and re-layouts  81.4 us (9%)
  waiting for transfers between devices  72.7 us (8%)
  loops' own time  18.7 us (2%)
  starting transfers between devices  8.85 us (1%)
    mul x6, other arithmetic, steering(): return (jnp.cos(phases) * factor, jnp.sin(phases) * factor)  221 us
    dot_general x6, matrix products, beam_power(): products = jnp.dot(weights, voltage, precision=highest)  127 us
    dot_general x1, matrix products, shifted_rows(): jnp.einsum('kcd,cbk->dbk', shift_cos, spec_real, precision=highest)  55.1 us
    dot_general x1, matrix products, shifted_rows(): jnp.einsum('kcd,cbk->dbk', shift_sin, spec_real, precision=highest)  54.8 us
    dot_general x1, matrix products, shifted_rows(): jnp.einsum('kcd,cbk->dbk', shift_sin, spec_imag, precision=highest)  54.4 us
    dot_general x1, matrix products, shifted_rows(): jnp.einsum('kcd,cbk->dbk', shift_cos, spec_imag, precision=highest)  54.2 us
    all_to_all x1, blocking collectives, exchange_in_pieces(): lax.all_to_all(slab, axis, split_axis=0, concat_axis=0, tiled=True)  49.1 us
    all_to_all x1, waiting for transfers between devices, exchange_in_pieces(): lax.all_to_all(slab, axis, split_axis=0, concat_axis=0, tiled=True)  44.6 us
  transfers between devices with their start and end apart: 2, of which 2 were waited for; matrix products, arithmetic and copies ran while one was open for 0% of the time, Pallas kernels for 0%

commit v1 on v0

v1 whole, which is shorter than its diff:
```python
import functools, math
import jax, jax.numpy as jnp, numpy as np
from jax import lax
from jax.experimental import pallas as pl
from jax.experimental.pallas import tpu as pltpu
from jax.sharding import PartitionSpec as P

FEEDS, CHANNELS, FRAMES, SIDE, BEAMS, GRID = 2048, 768, 64, 32, 1024, 64
F32, BF16 = jnp.float32, jnp.bfloat16


def halves(x):
    high = x.astype(BF16)
    return high, (x - high.astype(F32)).astype(BF16)


def steering_tables(channels):
    side = jnp.arange(SIDE, dtype=jnp.int32) - SIDE // 2
    cell = jnp.arange(GRID, dtype=jnp.int32)
    product = side[None, :, None] * cell[None, None, :] * (CHANNELS + channels)[:, None, None]
    phases = jnp.mod(product, GRID * CHANNELS).astype(F32) * (2.0 * math.pi / (GRID * CHANNELS))
    return jnp.concatenate([jnp.cos(phases), jnp.sin(phases)], axis=1)


def stacked(x):
    high, low = halves(x)
    return jnp.concatenate([high, low, high], axis=0)


def lane_sign(rows):
    lane = lax.broadcasted_iota(jnp.int32, (rows, 128), 1)
    return jnp.where(lane < FRAMES, 1.0, -1.0).astype(F32), lane < FRAMES


def beams_of(products, sign):
    return products[:SIDE] + pltpu.roll(products[SIDE:], FRAMES, 1) * sign


def beam_kernel(cells_ref, table_ref, volt_ref, out_ref, grid_ref, mid_ref):
    @pl.when(pl.program_id(0) == 0)
    def _():
        grid_ref[...] = jnp.zeros_like(grid_ref)

    def place(group, carry):
        for k in range(16):
            feed = group * 16 + k
            grid_ref[pl.ds(cells_ref[feed], 1), :] = volt_ref[group // 4, 0, pl.ds((group % 4) * 16 + k, 1), :]
        return carry

    lax.fori_loop(0, FEEDS // 16, place, 0)
    table_high, table_low = halves(table_ref[0])
    table = jnp.concatenate([table_high, table_high, table_low], axis=1)
    sign, low_lanes = lane_sign(SIDE)

    def over_columns(step, carry):
        pieces = []
        for k in range(2):
            row = step * 2 + k
            pieces.append(stacked(grid_ref[pl.ds(row * GRID, GRID), :]))
        products = jnp.dot(table, jnp.concatenate(pieces, axis=1), preferred_element_type=F32)
        for k in range(2):
            row = step * 2 + k
            mid_ref[pl.ds(row * SIDE, SIDE), :] = beams_of(products[:, k * 128 : (k + 1) * 128], sign)
        return carry

    lax.fori_loop(0, GRID // 2, over_columns, 0, unroll=4)
    for pair in range(SIDE // 2):
        pieces = [stacked(mid_ref[pl.ds(pair * 2 + k, GRID, stride=SIDE), :]) for k in range(2)]
        products = jnp.dot(table, jnp.concatenate(pieces, axis=1), preferred_element_type=F32)
        powers = []
        for k in range(2):
            beam = beams_of(products[:, k * 128 : (k + 1) * 128], sign)
            square = beam * beam
            powers.append(square + pltpu.roll(square, FRAMES, 1))
        out_ref[:, 0, pair, :] = jnp.where(low_lanes, powers[0], powers[1])


def beam_powers(feed_cells, tables, by_source):
    sources, chans = by_source.shape[:2]
    return pl.pallas_call(
        beam_kernel,
        out_shape=jax.ShapeDtypeStruct((SIDE, chans, SIDE // 2, 128), F32),
        grid_spec=pltpu.PrefetchScalarGridSpec(
            num_scalar_prefetch=1,
            grid=(chans,),
            in_specs=[
                pl.BlockSpec((1, 64, 64), lambda c, cells: (c, 0, 0)),
                pl.BlockSpec((sources, 1, 64, 128), lambda c, cells: (0, c, 0, 0)),
            ],
            out_specs=pl.BlockSpec((SIDE, 1, SIDE // 2, 128), lambda c, cells: (0, c, 0, 0)),
            scratch_shapes=[pltpu.VMEM((GRID * GRID, 128), F32), pltpu.VMEM((GRID * SIDE, 128), F32)],
        ),
        name="beam_powers",
    )(feed_cells, tables, by_source)


def dft_tables():
    t = np.arange(FRAMES)
    k = np.arange(1, 33)
    ang = 2.0 * np.pi * ((k[:, None] * t[None, :]) % FRAMES) / FRAMES
    fwd = np.concatenate([np.cos(ang), -np.sin(ang)], axis=0)
    weight = np.where(k == 32, 1.0, 2.0)[:, None]
    scale = 0.5 / (FRAMES * math.sqrt(CHANNELS)) / FEEDS
    inv = np.concatenate([np.cos(ang) * weight, -np.sin(ang) * weight], axis=0) * scale
    def pair(m):
        z = np.zeros_like(m)
        return np.block([[m, z], [z, m]]).astype(np.float32)
    return pair(fwd), pair(inv)


def split_const(m):
    high = m.astype(jnp.bfloat16)
    low = (m - high.astype(np.float32)).astype(jnp.bfloat16)
    return high, low


def shift_kernel(fwd_ref, inv_ref, delay_ref, pow_ref, out_ref, spec_ref, fold_ref, base_ref, turn_ref):
    nt = (((1,), (1,)), ((), ()))
    chans = pow_ref.shape[0]
    for pair in range(SIDE // 2):
        high, low = halves(pow_ref[:, pair, :])
        both = lax.dot_general(fwd_ref[...], high, nt, preferred_element_type=F32)
        spec = both[:128] + both[128:] + lax.dot_general(fwd_ref[:128], low, nt, preferred_element_type=F32)
        for odd in range(2):
            for part in range(2):
                rows = spec[(odd * 2 + part) * 32 : (odd * 2 + part + 1) * 32]
                at = pl.ds(part * 32 + pair * 2 + odd, 32, stride=64)
                spec_ref[0, at, :] = rows[:, :128]
                spec_ref[1, at, pl.ds(0, chans - 128)] = rows[:, 128:]
    angle = delay_ref[...].astype(F32) * (2.0 * math.pi / FRAMES)
    base_ref[0] = jnp.cos(angle)
    base_ref[1] = jnp.sin(angle)
    turn_ref[0] = base_ref[0]
    turn_ref[1] = base_ref[1]

    def one_bin(step, carry):
        at = pl.ds(pl.multiple_of(step * 64, 64), 64)
        spec = jnp.concatenate([spec_ref[0, at, :], spec_ref[1, at, pl.ds(0, chans - 128)]], axis=1)
        turned = jnp.concatenate([-spec[32:], spec[:32]], axis=0)
        total = None
        for value, part in ((spec, 0), (turned, 1)):
            high, low = halves(value)
            turn_high, turn_low = halves(turn_ref[part])
            both = jnp.dot(jnp.concatenate([high, low], axis=0), turn_high, preferred_element_type=F32)
            term = both[:64] + both[64:] + jnp.dot(high, turn_low, preferred_element_type=F32)
            total = term if total is None else total + term
        fold_ref[0, at, :] = total[:, :128]
        fold_ref[1, at, :] = total[:, 128:]
        real, imag = turn_ref[0], turn_ref[1]
        turn_ref[0] = real * base_ref[0] - imag * base_ref[1]
        turn_ref[1] = real * base_ref[1] + imag * base_ref[0]
        return carry

    lax.fori_loop(0, 32, one_bin, 0)
    for pair in range(SIDE // 2):
        for half in range(2):
            rows = [
                fold_ref[half, pl.ds(part * 32 + pair * 2 + odd, 32, stride=64), :]
                for odd in range(2) for part in range(2)
            ]
            high, low = halves(jnp.concatenate(rows, axis=0).T)
            series = (
                jnp.dot(high, inv_ref[:128], preferred_element_type=F32)
                + jnp.dot(high, inv_ref[128:], preferred_element_type=F32)
                + jnp.dot(low, inv_ref[:128], preferred_element_type=F32)
            )
            out_ref[pl.ds(half * 128, 128), pair, :] = series


def shifted_sums(powers, delays):
    fwd, inv = dft_tables()
    fwd = jnp.asarray(np.concatenate(split_const(fwd), axis=0))
    inv = jnp.asarray(np.concatenate(split_const(inv), axis=0))
    vmem = pl.BlockSpec(memory_space=pltpu.VMEM)
    chans, trials = delays.shape
    return pl.pallas_call(
        shift_kernel,
        out_shape=jax.ShapeDtypeStruct((trials, SIDE // 2, 128), F32),
        in_specs=[vmem] * 4,
        out_specs=vmem,
        scratch_shapes=[
            pltpu.VMEM((2, 2048, 128), F32),
            pltpu.VMEM((2, 2048, 128), F32),
            pltpu.VMEM((2, chans, trials), F32),
            pltpu.VMEM((2, chans, trials), F32),
        ],
        name="shifted_sums",
    )(fwd, inv, delays, powers)


def sum_kernel(in_ref, out_ref):
    for pair in range(SIDE // 2):
        total = in_ref[0, :, pair, :] + in_ref[1, :, pair, :] + in_ref[2, :, pair, :] + in_ref[3, :, pair, :]
        out_ref[:, 2 * pair, :] = total[:, :FRAMES]
        out_ref[:, 2 * pair + 1, :] = total[:, FRAMES:]


def summed(pieces):
    vmem = pl.BlockSpec(memory_space=pltpu.VMEM)
    return pl.pallas_call(
        sum_kernel,
        out_shape=jax.ShapeDtypeStruct((pieces.shape[1], SIDE, FRAMES), F32),
        in_specs=[vmem],
        out_specs=vmem,
        name="summed",
    )(pieces)


PIECES = 3


def body(voltages, feed_cells, delays):
    band_chans = voltages.shape[0]
    peers = lax.axis_size("feed")
    local_chans = band_chans // peers
    first = lax.axis_index("band") * band_chans + lax.axis_index("feed") * local_chans
    tables = steering_tables(first + jnp.arange(local_chans, dtype=jnp.int32))
    blocks = voltages.reshape(peers, local_chans, *voltages.shape[1:])
    span = local_chans // PIECES
    powers = []
    for piece in range(PIECES):
        at = slice(piece * span, (piece + 1) * span)
        moved = lax.all_to_all(blocks[:, at], "feed", 0, 0, tiled=True)
        powers.append(beam_powers(feed_cells, tables[at], moved))
    by_beam = lax.all_to_all(jnp.concatenate(powers, axis=1), "feed", 0, 0, tiled=True)
    partial = shifted_sums(by_beam.reshape(band_chans, SIDE // 2, 128), delays)
    owners = lax.axis_size("band")
    pieces = lax.all_to_all(partial.reshape(owners, -1, SIDE // 2, 128), "band", 0, 0, tiled=True)
    return summed(pieces)


def solution(mesh):
    placed = (P("band", "feed", None), P(), P("band", None))
    return jax.shard_map(
        body, mesh=mesh, in_specs=placed, out_specs=P("band", "feed", None), check_vma=False
    )
```

time: 862 us -> 216 us (0.25)
  matrix products: 355 us -> 0 us
  other arithmetic: 238 us -> 2.37 us
  local copies, waits for them, and re-layouts: 81.4 us -> 6.31 us
  waiting for transfers between devices: 72.7 us -> 0.01 us
  Pallas kernels: 0 us -> 71.6 us
  blocking collectives: 82.8 us -> 131 us
  loops' own time: 18.7 us -> 0 us
    dot_general x12 -> x0, matrix products: 355 us -> none  [the longest x6 127 us: beam_power(): products = jnp.dot(weights, voltage, precision=highest)]
    mul x7 -> x1, other arithmetic: 221 us -> 0.07 us  [steering_tables(): side[None, :, None] * cell[None, None, :]]
    all_to_all x2 -> x1, waiting for transfers between devices: 72.7 us -> 0.01 us  [body(): moved = lax.all_to_all(blocks[:, at], 'feed', 0, 0, tiled=True)]
    pallas_call x0 -> x5, Pallas kernels: none -> 71.6 us  [the longest x3 47.1 us: beam_powers(): pl.pallas_call(beam_kernel, out_shape=jax.ShapeDtypeStruct((SIDE, chans,...]
    all_to_all x2 -> x4, blocking collectives: 82.8 us -> 131 us  [the longest x2 68.5 us: body(): moved = lax.all_to_all(blocks[:, at], 'feed', 0, 0, tiled=True)]
    dynamic_update_slice x6 -> x0, local copies, waits for them, and re-layouts: 36.1 us -> none  [body(): powers = lax.map(beam_power, (channels, by_channel))]
    another operation x1 -> x0, loops' own time: 18.7 us -> none  [body(): powers = lax.map(beam_power, (channels, by_channel))]
    concatenate x2 -> x0, local copies, waits for them, and re-layouts: 9.19 us -> none  [the longest x1 5.92 us: shifted_rows(): return jnp.concatenate([out_real, out_imag], axis=2)]
  transfers between devices with their start and end apart: 2 -> 1, of which waited for: 2 -> 0; matrix products, arithmetic and copies ran while one was open for 0% -> 1% of each run, Pallas kernels for 0% -> 15%
where the time goes in v1:
time: 216 us
  blocking collectives  131 us (61%)
  Pallas kernels  71.6 us (33%)
  local copies, waits for them, and re-layouts  6.31 us (3%)
  starting transfers between devices  4.01 us (2%)
  other arithmetic  2.37 us (1%)
    all_to_all x2, blocking collectives, body(): moved = lax.all_to_all(blocks[:, at], 'feed', 0, 0, tiled=True)  68.5 us
    pallas_call x3, Pallas kernels, beam_powers(): pl.pallas_call(beam_kernel, out_shape=jax.ShapeDtypeStruct((SIDE, chans,...  47.1 us
    all_to_all x1, blocking collectives, body(): lax.all_to_all(partial.reshape(owners, -1, SIDE // 2, 128), 'band', 0, 0,...  34.6 us
    all_to_all x1, blocking collectives, body(): lax.all_to_all(jnp.concatenate(powers, axis=1), 'feed', 0, 0, tiled=True)  28.1 us
    pallas_call x1, Pallas kernels, shifted_sums(): pl.pallas_call(shift_kernel, out_shape=jax.ShapeDtypeStruct((trials, SIDE...  20.6 us
    slice x1, local copies, waits for them, and re-layouts, body(): moved = lax.all_to_all(blocks[:, at], 'feed', 0, 0, tiled=True)  4.96 us
  transfers between devices with their start and end apart: 1, of which 0 were waited for; matrix products, arithmetic and copies ran while one was open for 1% of the time, Pallas kernels for 15%

profile of v1, /device:TPU:1, one launch (start us, length us, event | category | flops | bytes accessed | tf_op | source)
XLA Modules:
  0.0 215.7 jit_solution(11070208640741037623)
XLA Ops:
  0.0 5.0 %fusion.9 = (f32[32,2,64,128]{3,2,1,0:T(8,128)S(1)}, f32[32,2,64,128]{3,2,1,0:T(8,128)S(1)}, f32[32,2,64,128]{3,2,1,0:T(8,128)}) fusion(f32[32,6,64,128]{3,2,1,0:T(8,128)} %bitcast.4), kind=kLoop, calls=%fused_computation.20 | loop fusion | bytes 12582912 | tf_op jit(solution)/shard_map/slice | solution.py:223
  5.0 37.8 %all_to_all.25.volt_ref = f32[32,2,64,128]{3,2,1,0:T(8,128)} all-to-all(f32[32,2,64,128]{3,2,1,0:T(8,128)S(1)} %get-tuple-element.5), channel_id=1, replica_groups=mesh['band'=4,'feed'=32] {'feed'}, dimensions={0} | all-to-all | bytes 4194304 | tf_op jit(solution)/shard_map/all_to_all | solution.py:223
  42.7 30.8 %all_to_all.26.volt_ref = f32[32,2,64,128]{3,2,1,0:T(8,128)} all-to-all(f32[32,2,64,128]{3,2,1,0:T(8,128)S(1)} %get-tuple-element.6), channel_id=1, replica_groups=mesh['band'=4,'feed'=32] {'feed'}, dimensions={0} | all-to-all | bytes 4194304 | tf_op jit(solution)/shard_map/all_to_all | solution.py:223
  73.5 4.0 %all-to-all-start.1 = ((f32[32,2,64,128]{3,2,1,0:T(8,128)}), f32[32,2,64,128]{3,2,1,0:T(8,128)S(1)}, u32[]{:S(2)}, u32[]{:S(2)}) async-start(f32[32,2,64,128]{3,2,1,0:T(8,128)} %get-tuple-element.7), calls=%async_computation.1 | async-start | bytes 4194304 | tf_op jit(solution)/shard_map/all_to_all | solution.py:223
  77.5 0.1 iota_multiply_fusion
  77.6 0.5 fusion.5
  78.1 0.7 fusion.8
  78.7 15.7 %beam_powers.3 = f32[32,2,16,128]{3,2,1,0:T(8,128)} custom-call(s32[4096]{0:T(1024)} %cells_ref.5, f32[2,64,64]{2,1,0:T(8,128)} %get-tuple-element.8.table_ref, f32[32,2,64,128]{3,2,1,0:T(8,128)} %all_to_all.25.volt_ref), custom_call_target="tpu_custom_call" | custom-call | tf_op jit(solution)/shard_map/beam_powers/pallas_call | solution.py:80
  94.4 0.0 copy-start.1
  94.4 15.8 %beam_powers.5 = f32[32,2,16,128]{3,2,1,0:T(8,128)} custom-call(s32[4096]{0:T(1024)} %cells_ref.5, f32[2,64,64]{2,1,0:T(8,128)} %get-tuple-element.9.table_ref, f32[32,2,64,128]{3,2,1,0:T(8,128)} %all_to_all.26.volt_ref), custom_call_target="tpu_custom_call" | custom-call | tf_op jit(solution)/shard_map/beam_powers/pallas_call | solution.py:80
  110.2 0.0 copy-start.2
  110.2 0.0 all-to-all-done.1.volt_ref
  110.2 0.0 copy-start
  110.2 1.3 copy-done
  111.6 15.7 %beam_powers.4 = f32[32,2,16,128]{3,2,1,0:T(8,128)} custom-call(s32[4096]{0:T(1024)} %cells_ref.5, f32[2,64,64]{2,1,0:T(8,128)} %get-tuple-element.10.table_ref, f32[32,2,64,128]{3,2,1,0:T(8,128)} %copy-done), custom_call_target="tpu_custom_call" | custom-call | tf_op jit(solution)/shard_map/beam_powers/pallas_call | solution.py:80
  127.2 0.0 copy-done.1
  127.2 0.0 copy-done.2
  127.2 1.1 pad_maximum_fusion
  128.4 28.1 %all_to_all.27 = f32[32,6,16,128]{3,2,1,0:T(8,128)} all-to-all(f32[32,6,16,128]{3,2,1,0:T(8,128)S(1)} %pad_maximum_fusion), channel_id=1, replica_groups=mesh['band'=4,'feed'=32] {'feed'}, dimensions={0} | all-to-all | bytes 3145728 | tf_op jit(solution)/shard_map/all_to_all | solution.py:225
  156.5 20.6 %shifted_sums.1 = f32[256,16,128]{2,1,0:T(8,128)} custom-call(bf16[256,128]{1,0:T(8,128)(2,1)} %constant.36.clone.fwd_ref, bf16[256,128]{1,0:T(8,128)(2,1)} %constant.37.clone.inv_ref, s32[192,256]{1,0:T(8,128)} %delay_ref.1, f32[192,16,128]{2,1,0:T(8,128)} %bitcast.5), custom_call_target="tpu_custom_call" | custom-call | tf_op jit(solution)/shard_map/shifted_sums/pallas_call | solution.py:176
  177.2 34.6 %all_to_all.28.in_ref = f32[4,64,16,128]{3,2,1,0:T(8,128)} all-to-all(f32[4,64,16,128]{3,2,1,0:T(8,128)} %bitcast.3), channel_id=1, replica_groups=mesh['band'=4,'feed'=32] {'band'}, dimensions={0} | all-to-all | bytes 4194304 | tf_op jit(solution)/shard_map/all_to_all | solution.py:228
  211.8 3.9 %summed.1 = f32[64,32,64]{2,1,0:T(8,128)} custom-call(f32[4,64,16,128]{3,2,1,0:T(8,128)} %all_to_all.28.in_ref), custom_call_target="tpu_custom_call" | custom-call | tf_op jit(solution)/shard_map/summed/pallas_call | solution.py:200
  (2 shorter events, 0.0 us)
Async XLA Ops:
  73.5 36.8 %all-to-all-start.1 = ((f32[32,2,64,128]{3,2,1,0:T(8,128)}), f32[32,2,64,128]{3,2,1,0:T(8,128)S(1)}, u32[]{:S(2)}, u32[]{:S(2)}) async-start(f32[32,2,64,128]{3,2,1,0:T(8,128)} %get-tuple-element.7), calls=%async_computation.1 | async-start | bytes 4194304 | tf_op jit(solution)/shard_map/all_to_all | solution.py:223
  94.4 32.8 %copy-start.1 = (f32[32,2,16,128]{3,2,1,0:T(8,128)S(1)}, f32[32,2,16,128]{3,2,1,0:T(8,128)}, u32[]{:S(2)}) copy-start(f32[32,2,16,128]{3,2,1,0:T(8,128)} %beam_powers.3) | copy-start | bytes 1572868
  110.2 17.0 %copy-start.2 = (f32[32,2,16,128]{3,2,1,0:T(8,128)S(1)}, f32[32,2,16,128]{3,2,1,0:T(8,128)}, u32[]{:S(2)}) copy-start(f32[32,2,16,128]{3,2,1,0:T(8,128)} %beam_powers.5) | copy-start | bytes 1572868
  110.2 1.3 copy-start

commit v2 on v1

--- a/solution.py
+++ b/solution.py
@@ -34,64 +34,6 @@
 
 def beams_of(products, sign):
     return products[:SIDE] + pltpu.roll(products[SIDE:], FRAMES, 1) * sign
-
-
-def beam_kernel(cells_ref, table_ref, volt_ref, out_ref, grid_ref, mid_ref):
-    @pl.when(pl.program_id(0) == 0)
-    def _():
-        grid_ref[...] = jnp.zeros_like(grid_ref)
-
-    def place(group, carry):
-        for k in range(16):
-            feed = group * 16 + k
-            grid_ref[pl.ds(cells_ref[feed], 1), :] = volt_ref[group // 4, 0, pl.ds((group % 4) * 16 + k, 1), :]
-        return carry
-
-    lax.fori_loop(0, FEEDS // 16, place, 0)
-    table_high, table_low = halves(table_ref[0])
-    table = jnp.concatenate([table_high, table_high, table_low], axis=1)
-    sign, low_lanes = lane_sign(SIDE)
-
-    def over_columns(step, carry):
-        pieces = []
-        for k in range(2):
-            row = step * 2 + k
-            pieces.append(stacked(grid_ref[pl.ds(row * GRID, GRID), :]))
-        products = jnp.dot(table, jnp.concatenate(pieces, axis=1), preferred_element_type=F32)
-        for k in range(2):
-            row = step * 2 + k
-            mid_ref[pl.ds(row * SIDE, SIDE), :] = beams_of(products[:, k * 128 : (k + 1) * 128], sign)
-        return carry
-
-    lax.fori_loop(0, GRID // 2, over_columns, 0, unroll=4)
-    for pair in range(SIDE // 2):
-        pieces = [stacked(mid_ref[pl.ds(pair * 2 + k, GRID, stride=SIDE), :]) for k in range(2)]
-        products = jnp.dot(table, jnp.concatenate(pieces, axis=1), preferred_element_type=F32)
-        powers = []
-        for k in range(2):
-            beam = beams_of(products[:, k * 128 : (k + 1) * 128], sign)
-            square = beam * beam
-            powers.append(square + pltpu.roll(square, FRAMES, 1))
-        out_ref[:, 0, pair, :] = jnp.where(low_lanes, powers[0], powers[1])
-
-
-def beam_powers(feed_cells, tables, by_source):
-    sources, chans = by_source.shape[:2]
-    return pl.pallas_call(
-        beam_kernel,
-        out_shape=jax.ShapeDtypeStruct((SIDE, chans, SIDE // 2, 128), F32),
-        grid_spec=pltpu.PrefetchScalarGridSpec(
-            num_scalar_prefetch=1,
-            grid=(chans,),
-            in_specs=[
-                pl.BlockSpec((1, 64, 64), lambda c, cells: (c, 0, 0)),
-                pl.BlockSpec((sources, 1, 64, 128), lambda c, cells: (0, c, 0, 0)),
-            ],
-            out_specs=pl.BlockSpec((SIDE, 1, SIDE // 2, 128), lambda c, cells: (0, c, 0, 0)),
-            scratch_shapes=[pltpu.VMEM((GRID * GRID, 128), F32), pltpu.VMEM((GRID * SIDE, 128), F32)],
-        ),
-        name="beam_powers",
-    )(feed_cells, tables, by_source)
 
 
 def dft_tables():
@@ -206,7 +148,147 @@
     )(pieces)
 
 
-PIECES = 3
+MESH = pl.DeviceIdType.MESH
+
+
+def feed_of_cell(feed_cells):
+    cells = feed_cells[:FEEDS]
+    line = jnp.arange(GRID, dtype=jnp.int32)[:, None]
+    rows = (cells[None, :] // GRID == line).astype(F32)
+    cols = jnp.where(cells[None, :] % GRID == line, jnp.arange(1, FEEDS + 1, dtype=jnp.int32)[None, :], 0).astype(F32)
+    found = lax.dot_general(rows, cols, (((1,), (1,)), ((), ())), precision=lax.Precision.HIGHEST)
+    found = jnp.round(found).astype(jnp.int32).reshape(GRID * GRID)
+    return jnp.where(found == 0, FEEDS, found - 1)
+
+
+def peer_at(me, step):
+    y, z, x = me // 8, (me // 2) % 4, me % 2
+    return ((y + step // 8) % 4) * 8 + ((z + (step // 2) % 4) % 4) * 2 + (x + step % 2) % 2
+
+
+def await_bytes(ref, sem):
+    pltpu.make_async_copy(ref, ref, sem).wait()
+
+
+def beams_of_grid(table, grid_ref, mid_ref, store):
+    sign, low_lanes = lane_sign(SIDE)
+
+    def over_columns(step, carry):
+        pieces = []
+        for k in range(2):
+            pieces.append(stacked(grid_ref[pl.ds(pl.multiple_of((step * 2 + k) * GRID, GRID), GRID), :]))
+        products = jnp.dot(table, jnp.concatenate(pieces, axis=1), preferred_element_type=F32)
+        for k in range(2):
+            at = pl.multiple_of((step * 2 + k) * SIDE, SIDE)
+            mid_ref[pl.ds(at, SIDE), :] = beams_of(products[:, k * 128 : (k + 1) * 128], sign)
+        return carry
+
+    lax.fori_loop(0, GRID // 2, over_columns, 0, unroll=4)
+    for pair in range(SIDE // 2):
+        pieces = [stacked(mid_ref[pl.ds(pair * 2 + k, GRID, stride=SIDE), :]) for k in range(2)]
+        products = jnp.dot(table, jnp.concatenate(pieces, axis=1), preferred_element_type=F32)
+        powers = []
+        for k in range(2):
+            beam = beams_of(products[:, k * 128 : (k + 1) * 128], sign)
+            square = beam * beam
+            powers.append(square + pltpu.roll(square, FRAMES, 1))
+        store(pair, jnp.where(low_lanes, powers[0], powers[1]))
+
+
+def gather_kernel(peers, chans, source_ref, table_ref, volt_ref, out_ref, *scratch):
+    land = scratch[:chans]
+    powers = scratch[chans : 2 * chans]
+    grid_ref, mid_ref, held, send_sem, land_sem, own_sem, pow_send, pow_land, out_sem = scratch[2 * chans :]
+    me = lax.axis_index("feed")
+    shard = FEEDS // peers
+    barrier = pltpu.get_barrier_semaphore()
+
+    def greet(step, carry):
+        pl.semaphore_signal(barrier, inc=1, device_id={"feed": peer_at(me, step)}, device_id_type=MESH)
+        return carry
+
+    lax.fori_loop(1, peers, greet, 0)
+    pl.semaphore_wait(barrier, peers - 1)
+    mine = pl.ds(pl.multiple_of(me * shard, shard), shard)
+    for c in range(chans):
+        def send(step, carry, c=c):
+            peer = peer_at(me, step)
+            pltpu.make_async_remote_copy(
+                src_ref=volt_ref.at[peer, c], dst_ref=land[c].at[mine], send_sem=send_sem.at[c],
+                recv_sem=land_sem.at[c], device_id={"feed": peer}, device_id_type=MESH,
+            ).start()
+            return carry
+
+        lax.fori_loop(1, peers, send, 0)
+        pltpu.make_async_copy(volt_ref.at[me, c], land[c].at[mine], own_sem.at[c]).start()
+        land[c][pl.ds(FEEDS, 8), :] = jnp.zeros((8, 128), F32)
+    arriving = pl.ds(0, FEEDS - shard)
+    for c in range(chans):
+        await_bytes(land[c].at[arriving], land_sem.at[c])
+        pltpu.make_async_copy(volt_ref.at[me, c], land[c].at[mine], own_sem.at[c]).wait()
+
+        def place(group, carry, c=c):
+            for k in range(16):
+                cell = group * 16 + k
+                grid_ref[pl.ds(cell, 1), :] = land[c][pl.ds(source_ref[cell], 1), :]
+            return carry
+
+        lax.fori_loop(0, GRID * GRID // 16, place, 0)
+        table_high, table_low = halves(table_ref[c])
+
+        def store(pair, power, c=c):
+            powers[c][:, pair, :] = power
+
+        beams_of_grid(jnp.concatenate([table_high, table_high, table_low], axis=1), grid_ref, mid_ref, store)
+        row = me * chans + c
+
+        def spread(step, carry, c=c):
+            peer = peer_at(me, step)
+            pltpu.make_async_remote_copy(
+                src_ref=powers[c].at[peer], dst_ref=held.at[me * chans + c], send_sem=pow_send.at[c],
+                recv_sem=pow_land, device_id={"feed": peer}, device_id_type=MESH,
+            ).start()
+            return carry
+
+        lax.fori_loop(1, peers, spread, 0)
+        held[row] = powers[c][me]
+    await_bytes(held.at[pl.ds(0, (peers - 1) * chans)], pow_land)
+    copy = pltpu.make_async_copy(held, out_ref, out_sem)
+    copy.start()
+    for c in range(chans):
+        await_bytes(land[c].at[arriving], send_sem.at[c])
+        await_bytes(powers[c].at[pl.ds(0, peers - 1)], pow_send.at[c])
+    copy.wait()
+
+
+def gathered_powers(source, tables, blocks):
+    peers, chans, shard, lanes = blocks.shape
+    kernel = functools.partial(gather_kernel, peers, chans)
+    return pl.pallas_call(
+        kernel,
+        out_shape=jax.ShapeDtypeStruct((peers * chans, SIDE // 2, 128), F32),
+        in_specs=[
+            pl.BlockSpec(memory_space=pltpu.SMEM),
+            pl.BlockSpec(memory_space=pltpu.VMEM),
+            pl.BlockSpec(memory_space=pl.ANY),
+        ],
+        out_specs=pl.BlockSpec(memory_space=pl.ANY),
+        scratch_shapes=[pltpu.VMEM((FEEDS + 8, 128), F32)] * chans
+        + [pltpu.VMEM((SIDE, SIDE // 2, 128), F32)] * chans
+        + [
+            pltpu.VMEM((GRID * GRID, 128), F32),
+            pltpu.VMEM((GRID * SIDE, 128), F32),
+            pltpu.VMEM((peers * chans, SIDE // 2, 128), F32),
+            pltpu.SemaphoreType.DMA((chans,)),
+            pltpu.SemaphoreType.DMA((chans,)),
+            pltpu.SemaphoreType.DMA((chans,)),
+            pltpu.SemaphoreType.DMA((chans,)),
+            pltpu.SemaphoreType.DMA,
+            pltpu.SemaphoreType.DMA,
+        ],
+        compiler_params=pltpu.CompilerParams(collective_id=0, has_side_effects=True),
+        name="gathered_powers",
+    )(source, tables, blocks)
 
 
 def body(voltages, feed_cells, delays):
@@ -216,14 +298,8 @@
     first = lax.axis_index("band") * band_chans + lax.axis_index("feed") * local_chans
     tables = steering_tables(first + jnp.arange(local_chans, dtype=jnp.int32))
     blocks = voltages.reshape(peers, local_chans, *voltages.shape[1:])
-    span = local_chans // PIECES
-    powers = []
-    for piece in range(PIECES):
-        at = slice(piece * span, (piece + 1) * span)
-        moved = lax.all_to_all(blocks[:, at], "feed", 0, 0, tiled=True)
-        powers.append(beam_powers(feed_cells, tables[at], moved))
-    by_beam = lax.all_to_all(jnp.concatenate(powers, axis=1), "feed", 0, 0, tiled=True)
-    partial = shifted_sums(by_beam.reshape(band_chans, SIDE // 2, 128), delays)
+    by_beam = gathered_powers(feed_of_cell(feed_cells), tables, blocks)
+    partial = shifted_sums(by_beam, delays)
     owners = lax.axis_size("band")
     pieces = lax.all_to_all(partial.reshape(owners, -1, SIDE // 2, 128), "band", 0, 0, tiled=True)
     return summed(pieces)

time: 216 us -> 161 us (0.75)
  blocking collectives: 131 us -> 34.5 us
  Pallas kernels: 71.6 us -> 122 us
  local copies, waits for them, and re-layouts: 6.31 us -> 0.68 us
  starting transfers between devices: 4.01 us -> 0 us
    all_to_all x3 -> x0, blocking collectives: 96.6 us -> none  [the longest x2 68.5 us: body(): moved = lax.all_to_all(blocks[:, at], 'feed', 0, 0, tiled=True)]
    pallas_call x3 -> x1, Pallas kernels: 47.1 us -> 97.4 us  [gathered_powers(): pl.pallas_call(kernel, out_shape=jax.ShapeDtypeStruct((peers * chans, SID...]
    slice x1 -> x0, local copies, waits for them, and re-layouts: 4.96 us -> none  [body(): moved = lax.all_to_all(blocks[:, at], 'feed', 0, 0, tiled=True)]
    all_to_all x1 -> x0, starting transfers between devices: 4.01 us -> none  [body(): moved = lax.all_to_all(blocks[:, at], 'feed', 0, 0, tiled=True)]
  transfers between devices with their start and end apart: 1 -> 0, of which waited for: 0 -> 0; matrix products, arithmetic and copies ran while one was open for 1% -> 0% of each run, Pallas kernels for 15% -> 0%
where the time goes in v2:
time: 161 us; the launch traced here: 160 us
  Pallas kernels  122 us (76%)
  blocking collectives  34.5 us (21%)
  other arithmetic  2.66 us (2%)
    pallas_call x1, Pallas kernels, gathered_powers(): pl.pallas_call(kernel, out_shape=jax.ShapeDtypeStruct((peers * chans, SID...  97.4 us
    all_to_all x1, blocking collectives, body(): lax.all_to_all(partial.reshape(owners, -1, SIDE // 2, 128), 'band', 0, 0,...  34.5 us
    pallas_call x1, Pallas kernels, shifted_sums(): pl.pallas_call(shift_kernel, out_shape=jax.ShapeDtypeStruct((trials, SIDE...  20.6 us
    pallas_call x1, Pallas kernels, summed(): pl.pallas_call(sum_kernel, out_shape=jax.ShapeDtypeStruct((pieces.shape[1...  3.87 us

profile of v2, /device:TPU:1, one launch (start us, length us, event | category | flops | bytes accessed | tf_op | source)
XLA Modules:
  0.0 160.2 jit_solution(7419417696101413533)
XLA Ops:
  0.0 0.7 add_select_fusion.3
  0.7 0.1 iota_multiply_fusion
  0.8 0.7 add_select_fusion.2
  1.5 0.5 add_select_fusion.1
  2.0 0.7 select_n.34.source_ref
  2.7 0.5 fusion.12
  3.2 0.7 pad_maximum_fusion.table_ref
  3.9 97.4 %gathered_powers.1.pow_ref = f32[192,16,128]{2,1,0:T(8,128)} custom-call(s32[4096]{0:T(1024)} %select_n.34.source_ref, f32[6,64,64]{2,1,0:T(8,128)} %pad_maximum_fusion.table_ref, f32[32,6,64,128]{3,2,1,0:T(8,128)} %bitcast.3), custom_call_target="tpu_custom_call" | custom-call | tf_op jit(solution)/shard_map/gathered_powers/pallas_call | solution.py:267
  101.2 20.6 %shifted_sums.1 = f32[256,16,128]{2,1,0:T(8,128)} custom-call(bf16[256,128]{1,0:T(8,128)(2,1)} %constant.69.clone.fwd_ref, bf16[256,128]{1,0:T(8,128)(2,1)} %constant.70.clone.inv_ref, s32[192,256]{1,0:T(8,128)} %delay_ref.1, f32[192,16,128]{2,1,0:T(8,128)} %gathered_powers.1.pow_ref), custom_call_target="tpu_custom_call" | custom-call | tf_op jit(solution)/shard_map/shifted_sums/pallas_call | solution.py:118
  121.9 34.5 %all_to_all.5.in_ref = f32[4,64,16,128]{3,2,1,0:T(8,128)} all-to-all(f32[4,64,16,128]{3,2,1,0:T(8,128)} %bitcast.2), channel_id=1, replica_groups=mesh['band'=4,'feed'=32] {'band'}, dimensions={0} | all-to-all | bytes 4194304 | tf_op jit(solution)/shard_map/all_to_all | solution.py:304
  156.4 3.9 %summed.1 = f32[64,32,64]{2,1,0:T(8,128)} custom-call(f32[4,64,16,128]{3,2,1,0:T(8,128)} %all_to_all.5.in_ref), custom_call_target="tpu_custom_call" | custom-call | tf_op jit(solution)/shard_map/summed/pallas_call | solution.py:142
  (2 shorter events, 0.0 us)
